TPU v7x, 512 devices: a whole 4x4x16 slice. The times are simulated.
512 devices in a mesh: rep: 4 (over y), exp: 128 (over x, z, core).
Axes of the slice: x: 4, y: 4, z: 16, core: 2. Of those that a mesh axis runs over, the one named last changes fastest.
Arguments:
- tokens: bfloat16 [16384, 3584], P(('rep', 'exp')), parts along dimension 0, may hold values from -6 to 6
- expert_ids: int32 [16384, 8], P(('rep', 'exp')), parts along dimension 0, may hold values from 0 to 383, all different within a row; in each aligned block of 32 rows (0 to 31, 32 to 63, ...) at most 2 rows name the same one
- gate_scores: float32 [16384, 8], P(('rep', 'exp')), parts along dimension 0, may hold values from 0.02 to 0.4
- gate_weight: bfloat16 [3584, 16384], P(None, 'exp'), may hold values from -0.09375 to 0.09375
- up_weight: bfloat16 [3584, 16384], P(None, 'exp'), may hold values from -0.09375 to 0.09375
- down_weight: bfloat16 [16384, 3584], P('exp'), may hold values from -0.125 to 0.125
Outputs:
- combined: bfloat16 [16384, 3584], P(('rep', 'exp')), parts along dimension 0
- expert_load: float32 [1536], P('rep'), parts along dimension 0
There are 4 independent parts, one for each index of `rep`. A program takes and returns all parts, laid end to end along the dimension named above; an argument that names none is the same for every part. Nothing has to cross between parts.
Inputs may be any that keep to these rules, and one draw needn't show every extreme that they name: `expert_ids`: each row names 8 different experts. Among the rows of one device no expert is named by more than 2 rows, a bound that some block reaches.
All inputs are finite; a program needn't handle non-finite values.
Results may differ from a plain program's by a relative error of at most 0.0057.
Values may be sent and summed in bfloat16 or wider, within the bound.
No kernel may reach another device: no remote copies, remote signals or barrier semaphores. Data moves between devices by JAX's collectives and lax.ppermute only.
A program may use at most 64 MiB of HBM per device.

v0:
```python
import jax
import jax.numpy as jnp
from jax import lax
from jax.sharding import PartitionSpec as P

FF = 2048
EXPERTS_ALL = 384
EXPERTS = 8
CAP = 2


def expert_rows(arrived, gate_weight, up_weight, down_weight):
    flat_rows = arrived.reshape(-1, arrived.shape[-1])
    gate_act = jnp.dot(flat_rows, gate_weight, preferred_element_type=jnp.float32)
    up_act = jnp.dot(flat_rows, up_weight, preferred_element_type=jnp.float32)
    hidden = (jax.nn.silu(gate_act) * up_act).astype(jnp.bfloat16)
    partial_value = jnp.dot(hidden, down_weight, preferred_element_type=jnp.float32).astype(
        jnp.bfloat16
    )
    return partial_value.reshape(arrived.shape)


def shards(tokens, expert_ids, gate_scores, gate_weight, up_weight, down_weight):
    dev_count = lax.axis_size("exp")
    hid_dev = gate_weight.shape[1]
    spread = FF // hid_dev
    tok_rows = tokens.shape[0]
    feat_width = tokens.shape[1]
    matches = expert_ids[:, :, None] == jnp.arange(EXPERTS_ALL, dtype=jnp.int32)[None, None, :]
    onehot = jnp.where(matches, 1.0, 0.0).astype(jnp.float32)
    routed_mass = jnp.einsum("tk,tke->e", gate_scores, onehot, precision=lax.Precision.HIGHEST)
    expert_load = lax.psum(routed_mass, "exp")
    window_match = matches[:, :, :EXPERTS]
    win_hits = jnp.any(window_match, axis=1)
    win_gate = jnp.sum(jnp.where(window_match, gate_scores[:, :, None], 0.0), axis=1)
    position = jnp.cumsum(win_hits.astype(jnp.int32), axis=0) - 1
    slot_ids = jnp.arange(CAP, dtype=jnp.int32)
    placed = win_hits[:, :, None] & (position[:, :, None] == slot_ids[None, None, :])
    placing = placed.reshape(tok_rows, EXPERTS * CAP)
    picker = jnp.where(placing.T, 1.0, 0.0).astype(jnp.bfloat16)
    outgoing = jnp.dot(picker, tokens, preferred_element_type=jnp.float32).astype(jnp.bfloat16)
    outgoing = jnp.broadcast_to(
        outgoing.reshape(EXPERTS, 1, CAP, feat_width), (EXPERTS, spread, CAP, feat_width)
    )
    outgoing = outgoing.reshape(dev_count, CAP, feat_width)
    arrived = lax.all_to_all(outgoing, "exp", split_axis=0, concat_axis=0, tiled=True)
    returned = lax.all_to_all(
        expert_rows(arrived, gate_weight, up_weight, down_weight),
        "exp",
        split_axis=0,
        concat_axis=0,
        tiled=True,
    )
    summed = jnp.sum(returned.reshape(EXPERTS, spread, CAP, feat_width), axis=1, dtype=jnp.float32)
    summed = summed.reshape(EXPERTS * CAP, feat_width)
    weights_slot = jnp.where(placed, win_gate[:, :, None], 0.0).reshape(tok_rows, EXPERTS * CAP)
    combined = jnp.dot(weights_slot, summed, precision=lax.Precision.HIGHEST).astype(jnp.bfloat16)
    return (combined, expert_load)


def solution(mesh):
    return jax.shard_map(
        shards,
        mesh=mesh,
        in_specs=(
            P(("rep", "exp"), None),
            P(("rep", "exp"), None),
            P(("rep", "exp"), None),
            P(None, "exp"),
            P(None, "exp"),
            P("exp", None),
        ),
        out_specs=(P(("rep", "exp"), None), P("rep")),
        check_vma=False,
    )
```

profile of v0, /device:TPU:1, one launch (start us, length us, event | category | flops | bytes accessed | tf_op | source)
XLA Modules:
  0.0 458.2 jit_solution(18036229864362332462)
XLA Ops:
  0.6 0.0 copy-start
  0.7 0.1 eq.45
  0.7 1.0 iota_compare_fusion
  1.8 0.1 copy.23
  1.8 0.1 reduce_window_sum.11
  1.9 0.1 copy.24
  2.0 1.2 convolution_convert_fusion.1
  3.2 0.9 broadcast_in_dim.61
  4.2 108.1 %all_to_all.10 = bf16[128,2,3584]{2,1,0:T(2,128)(2,1)} all-to-all(bf16[128,2,3584]{2,1,0:T(2,128)(2,1)S(1)} %bitcast.21), channel_id=1, replica_groups=mesh['rep'=4,'exp'=128] {'exp'}, dimensions={0} | all-to-all | bytes 3670016 | tf_op jit(solution)/shard_map/all_to_all | solution.py:46
  112.3 4.1 reshape.38
  116.4 1.8 fusion.25
  118.2 0.0 copy-done
  118.2 3.6 convolution_convert_fusion
  121.8 4.7 %reshape.39 = bf16[128,2,3584]{2,1,0:T(2,128)(2,1)} reshape(bf16[256,3584]{1,0:T(8,128)(2,1)} %convolution_convert_fusion) | data formatting | bytes 3670016 | tf_op jit(solution)/shard_map/reshape | solution.py:20
  126.6 0.0 copy-start.1
  126.6 0.0 copy-start.2
  126.6 8.9 %all-to-all-start.1 = ((bf16[128,2,3584]{2,1,0:T(2,128)(2,1)}), bf16[128,2,3584]{2,1,0:T(2,128)(2,1)S(1)}, u32[]{:S(2)}, u32[]{:S(2)}) async-start(bf16[128,2,3584]{2,1,0:T(2,128)(2,1)} %reshape.39), calls=%async_computation.1 | async-start | bytes 3670016 | tf_op jit(solution)/shard_map/all_to_all | solution.py:47
  135.4 0.0 copy-done.1
  135.4 0.0 copy-done.2
  135.4 1.5 fusion.4
  137.0 318.4 %psum.7 = f32[384]{0:T(512)} all-reduce(f32[384]{0:T(512)S(1)} %fusion.4), channel_id=1, replica_groups=mesh['rep'=4,'exp'=128] {'exp'}, use_global_device_ids=true, to_apply=%region_4.5 | all-reduce | flops 384 | bytes 3072 | tf_op jit(solution)/shard_map/psum | solution.py:32
  455.4 0.0 all-to-all-done.1
  455.4 1.5 convert_reduce_fusion
  456.9 1.3 fusion
  (10 shorter events, 0.1 us)
Async XLA Ops:
  0.6 117.6 %copy-start = (bf16[128,3584]{1,0:T(8,128)(2,1)S(1)}, bf16[128,3584]{1,0:T(8,128)(2,1)}, u32[]{:S(2)}) copy-start(bf16[128,3584]{1,0:T(8,128)(2,1)} %param.11) | copy-start | bytes 2752516
  126.6 8.9 %copy-start.1 = (s32[32,8]{0,1:T(8,128)S(1)}, s32[32,8]{0,1:T(8,128)}, u32[]{:S(2)}) copy-start(s32[32,8]{0,1:T(8,128)} %param.7) | copy-start | bytes 3076
  126.6 8.9 %copy-start.2 = (f32[32,8]{0,1:T(8,128)S(1)}, f32[32,8]{0,1:T(8,128)}, u32[]{:S(2)}) copy-start(f32[32,8]{0,1:T(8,128)} %param.8) | copy-start | bytes 3076
  126.6 328.9 %all-to-all-start.1 = ((bf16[128,2,3584]{2,1,0:T(2,128)(2,1)}), bf16[128,2,3584]{2,1,0:T(2,128)(2,1)S(1)}, u32[]{:S(2)}, u32[]{:S(2)}) async-start(bf16[128,2,3584]{2,1,0:T(2,128)(2,1)} %reshape.39), calls=%async_computation.1 | async-start | bytes 3670016 | tf_op jit(solution)/shard_map/all_to_all | solution.py:47
where the time goes:
time: 459 us; the launch traced here: 458 us
  blocking collectives  427 us (93%)
  local copies, waits for them, and re-layouts  10.1 us (2%)
  matrix products  9.36 us (2%)
  starting transfers between devices  8.85 us (2%)
    psum x1, blocking collectives, shards(): expert_load = lax.psum(routed_mass, 'exp')  318 us
    all_to_all x1, blocking collectives, shards(): lax.all_to_all(outgoing, 'exp', split_axis=0, concat_axis=0, tiled=True)  108 us
  transfers between devices with their start and end apart: 1, of which 0 were waited for; matrix products, arithmetic and copies ran while one was open for 0% of the time, Pallas kernels for 0%

commit v1 on v0

--- a/solution.py
+++ b/solution.py
@@ -7,6 +7,12 @@
 EXPERTS_ALL = 384
 EXPERTS = 8
 CAP = 2
+
+
+def _save_clusters(mine):
+    carry_in = lax.all_gather(mine, axis_name="exp")
+    y1 = jnp.sum(carry_in, axis=0)
+    return y1
 
 
 def expert_rows(arrived, gate_weight, up_weight, down_weight):
@@ -29,7 +35,7 @@
     matches = expert_ids[:, :, None] == jnp.arange(EXPERTS_ALL, dtype=jnp.int32)[None, None, :]
     onehot = jnp.where(matches, 1.0, 0.0).astype(jnp.float32)
     routed_mass = jnp.einsum("tk,tke->e", gate_scores, onehot, precision=lax.Precision.HIGHEST)
-    expert_load = lax.psum(routed_mass, "exp")
+    expert_load = _save_clusters(routed_mass)
     window_match = matches[:, :, :EXPERTS]
     win_hits = jnp.any(window_match, axis=1)
     win_gate = jnp.sum(jnp.where(window_match, gate_scores[:, :, None], 0.0), axis=1)

time: 459 us -> 311 us (0.68)
  blocking collectives: 427 us -> 278 us
    psum x1 -> x0, blocking collectives: 318 us -> none  [shards(): expert_load = lax.psum(routed_mass, 'exp')]
    all_gather x0 -> x1, blocking collectives: none -> 170 us  [_save_clusters(): carry_in = lax.all_gather(mine, axis_name='exp')]
  transfers between devices with their start and end apart: 1 -> 1, of which waited for: 0 -> 0; matrix products, arithmetic and copies ran while one was open for 0% -> 1% of each run, Pallas kernels for 0% -> 0%
where the time goes in v1:
time: 311 us
  blocking collectives  278 us (89%)
  local copies, waits for them, and re-layouts  10.1 us (3%)
  matrix products  9.34 us (3%)
  starting transfers between devices  8.86 us (3%)
  other arithmetic  3.31 us (1%)
    all_gather x1, blocking collectives, _save_clusters(): carry_in = lax.all_gather(mine, axis_name='exp')  170 us
    all_to_all x1, blocking collectives, shards(): lax.all_to_all(outgoing, 'exp', split_axis=0, concat_axis=0, tiled=True)  108 us
    all_to_all x1, starting transfers between devices, shards(): lax.all_to_all(expert_rows(arrived, gate_weight, up_weight, down_weight),...  8.86 us
  transfers between devices with their start and end apart: 1, of which 0 were waited for; matrix products, arithmetic and copies ran while one was open for 1% of the time, Pallas kernels for 0%

profile of v1, /device:TPU:1, one launch (start us, length us, event | category | flops | bytes accessed | tf_op | source)
XLA Modules:
  0.0 310.5 jit_solution(9572112601727017249)
XLA Ops:
  0.6 0.0 copy-start
  0.7 0.1 eq.45
  0.7 1.0 iota_compare_fusion
  1.8 0.1 copy.23
  1.8 0.1 reduce_window_sum.11
  1.9 0.1 copy.24
  2.0 1.2 convolution_convert_fusion.1
  3.2 0.9 broadcast_in_dim.61
  4.2 108.1 %all_to_all.10 = bf16[128,2,3584]{2,1,0:T(2,128)(2,1)} all-to-all(bf16[128,2,3584]{2,1,0:T(2,128)(2,1)S(1)} %bitcast.23), channel_id=1, replica_groups=mesh['rep'=4,'exp'=128] {'exp'}, dimensions={0} | all-to-all | bytes 3670016 | tf_op jit(solution)/shard_map/all_to_all | solution.py:52
  112.3 4.1 %reshape.38 = bf16[256,3584]{1,0:T(8,128)(2,1)S(1)} reshape(bf16[128,2,3584]{2,1,0:T(2,128)(2,1)} %all_to_all.10) | data formatting | bytes 3670016 | tf_op jit(solution)/shard_map/reshape | solution.py:19
  116.4 1.8 fusion.25
  118.2 0.0 copy-done
  118.2 3.6 %convolution_convert_fusion = bf16[256,3584]{1,0:T(8,128)(2,1)} fusion(bf16[128,3584]{1,0:T(8,128)(2,1)S(1)} %copy-done, bf16[256,3584]{1,0:T(8,128)(2,1)S(1)} %reshape.38, bf16[3584,128]{1,0:T(8,128)(2,1)} %param.10, f32[256,128]{1,0:T(8,128)S(1)} %fusion.25), kind=kOutput, calls=%fused_computation | convolution fusion | flops 470876160 | bytes 5636096 | tf_op jit(solution)/shard_map/dot_general | solution.py:23
  121.8 4.7 %reshape.39 = bf16[128,2,3584]{2,1,0:T(2,128)(2,1)} reshape(bf16[256,3584]{1,0:T(8,128)(2,1)} %convolution_convert_fusion) | data formatting | bytes 3670016 | tf_op jit(solution)/shard_map/reshape | solution.py:26
  126.6 0.0 copy-start.1
  126.6 0.0 copy-start.2
  126.6 8.9 %all-to-all-start.1 = ((bf16[128,2,3584]{2,1,0:T(2,128)(2,1)}), bf16[128,2,3584]{2,1,0:T(2,128)(2,1)S(1)}, u32[]{:S(2)}, u32[]{:S(2)}) async-start(bf16[128,2,3584]{2,1,0:T(2,128)(2,1)} %reshape.39), calls=%async_computation.1 | async-start | bytes 3670016 | tf_op jit(solution)/shard_map/all_to_all | solution.py:53
  135.4 0.0 copy-done.1
  135.4 0.0 copy-done.2
  135.4 1.5 fusion.4
  136.9 170.1 %all-gather.1 = f32[128,1,384]{2,1,0:T(1,128)S(1)} all-gather(f32[1,1,384]{2,1,0:T(1,128)S(1)} %fusion.4), channel_id=2, replica_groups=mesh['rep'=4,'exp'=128] {'exp'}, dimensions={0}, use_global_device_ids=true | all-gather | bytes 198144 | tf_op jit(solution)/shard_map/all_gather | solution.py:13
  307.0 0.8 reduce_sum.29
  307.8 0.0 all-to-all-done.1
  307.8 1.5 convert_reduce_fusion
  309.3 1.3 fusion
  (10 shorter events, 0.1 us)
Async XLA Ops:
  0.6 117.6 %copy-start = (bf16[128,3584]{1,0:T(8,128)(2,1)S(1)}, bf16[128,3584]{1,0:T(8,128)(2,1)}, u32[]{:S(2)}) copy-start(bf16[128,3584]{1,0:T(8,128)(2,1)} %param.11) | copy-start | bytes 2752516
  126.6 8.9 %copy-start.1 = (s32[32,8]{0,1:T(8,128)S(1)}, s32[32,8]{0,1:T(8,128)}, u32[]{:S(2)}) copy-start(s32[32,8]{0,1:T(8,128)} %param.7) | copy-start | bytes 3076
  126.6 8.9 %copy-start.2 = (f32[32,8]{0,1:T(8,128)S(1)}, f32[32,8]{0,1:T(8,128)}, u32[]{:S(2)}) copy-start(f32[32,8]{0,1:T(8,128)} %param.8) | copy-start | bytes 3076
  126.6 181.2 %all-to-all-start.1 = ((bf16[128,2,3584]{2,1,0:T(2,128)(2,1)}), bf16[128,2,3584]{2,1,0:T(2,128)(2,1)S(1)}, u32[]{:S(2)}, u32[]{:S(2)}) async-start(bf16[128,2,3584]{2,1,0:T(2,128)(2,1)} %reshape.39), calls=%async_computation.1 | async-start | bytes 3670016 | tf_op jit(solution)/shard_map/all_to_all | solution.py:53
